TPU v7x, 32 devices: a whole 2x2x4 slice. The times are simulated.
32 devices in a mesh: dp: 16 (over z, y, x), tensor: 2 (over core).
Axes of the slice: x: 2, y: 2, z: 4, core: 2. Of those that a mesh axis runs over, the one named last changes fastest.
Arguments:
- tokens: bfloat16 [2048, 768], P('dp'), may hold values from -6 to 6
- seq_ids: int32 [2048], P('dp'), may hold values from 0 to 127, as said below
- routes: int32 [2048, 2], P('dp'), may hold values from 0 to 3, all different within a row; in each aligned block of 128 rows (0 to 127, 128 to 255, ...) at most 80 rows name the same one
- gain_attn: float32 [768], replicated, may hold values from 0.25 to 1.75
- w_query: bfloat16 [768, 768], P(None, 'tensor'), may hold values from -0.21875 to 0.21875
- w_key: bfloat16 [768, 768], P(None, 'tensor'), may hold values from -0.21875 to 0.21875
- w_value: bfloat16 [768, 768], P(None, 'tensor'), may hold values from -0.21875 to 0.21875
- w_attn_out: bfloat16 [768, 768], P('tensor'), may hold values from -0.625 to 0.625
- rel_bias: float32 [12, 32], P('tensor'), may hold values from -2.5 to 2.5
- gain_ffn: float32 [768], replicated, may hold values from 0.25 to 1.75
- w_router: bfloat16 [768, 4], replicated, may hold values from -0.145 to 0.145
- expert_in: bfloat16 [16, 768, 768], P('dp', None, 'tensor'), may hold values from -0.21875 to 0.21875
- expert_out: bfloat16 [16, 768, 768], P('dp', 'tensor'), may hold values from -1.75 to 1.75
- cotangent: bfloat16 [2048, 768], P('dp'), may hold values from -6 to 6
Outputs:
- output: bfloat16 [2048, 768], P('dp')
- grad_tokens: float32 [2048, 768], P('dp')
- grad_gain_attn: float32 [768], replicated
- grad_w_query: float32 [768, 768], P(None, 'tensor')
- grad_w_key: float32 [768, 768], P(None, 'tensor')
- grad_w_value: float32 [768, 768], P(None, 'tensor')
- grad_w_attn_out: float32 [768, 768], P('tensor')
- grad_rel_bias: float32 [12, 32], P('tensor')
- grad_gain_ffn: float32 [768], replicated
- grad_w_router: float32 [768, 4], replicated
- grad_expert_in: float32 [16, 768, 768], P('dp', None, 'tensor')
- grad_expert_out: float32 [16, 768, 768], P('dp', 'tensor')
Inputs may be any that keep to these rules, and one draw needn't show every extreme that they name: `seq_ids`: in each device's 128 rows the sequence number starts at 0 and rises by 0 or 1 from row to row; equal numbers form one sequence; in every draw some device holds a single sequence of 128 rows, and some device holds 128 sequences of one row. `routes`: the 2 experts of a row differ; within the 128 rows of one device no expert is named more than 80 times, and in every draw some expert is named exactly 80 times there.
All inputs are finite; a program needn't handle non-finite values.
Results may differ from a plain program's by a relative error of at most 0.017.
Values may be sent and summed in bfloat16 or wider, within the bound.
No kernel may reach another device: no remote copies, remote signals or barrier semaphores. Data moves between devices by JAX's collectives and lax.ppermute only.
A program may use at most 128 MiB of HBM per device.

v0:
```python
import jax
import jax.numpy as jnp
import numpy as np
from jax import lax
from jax.sharding import PartitionSpec as P

HEAD_DIM = 64
TOP = 2
REACH = 64
eps_norm = 1e-06


def bucket_matrix(length, buckets, max_reach):
    exact_span = buckets // 2
    distance = np.arange(length)
    log_ratio = np.log(np.maximum(distance, exact_span) / exact_span) / np.log(
        max_reach / exact_span
    )
    coarse = exact_span + np.floor(log_ratio * (buckets - exact_span)).astype(np.int64)
    bucket_of = np.where(distance < exact_span, distance, np.minimum(coarse, buckets - 1))
    offset = np.maximum(distance[:, None] - distance[None, :], 0)
    return bucket_of[offset].astype(np.int32)


def gelu_tanh(values):
    return jax.nn.gelu(values, approximate=True)


def rms_forward(values, gain_vec):
    inv_rms = lax.rsqrt(jnp.mean(values * values, axis=-1, keepdims=True) + eps_norm)
    return (values * inv_rms * gain_vec, inv_rms)


def rms_backward(grad_normed, values, inv_rms, gain_vec):
    scaled = grad_normed * gain_vec
    inv_cubed = inv_rms * inv_rms * inv_rms
    grad_values = inv_rms * scaled - values * inv_cubed * jnp.mean(
        scaled * values, axis=-1, keepdims=True
    )
    grad_gain = jnp.sum(grad_normed * values * inv_rms, axis=0)
    return (grad_values, grad_gain)


def slot_of(route_ids, experts, capacity):
    count_all = route_ids.shape[0] * route_ids.shape[1]
    flat_ids = route_ids.reshape(-1)
    expert_hot = (flat_ids[:, None] == jnp.arange(experts, dtype=jnp.int32)[None, :]).astype(
        jnp.bfloat16
    )
    order_ids = jnp.arange(count_all, dtype=jnp.int32)
    earlier = (order_ids[:, None] > order_ids[None, :]).astype(jnp.bfloat16)
    before = jnp.dot(earlier, expert_hot, preferred_element_type=jnp.float32)
    rank_in = jnp.sum(before * expert_hot.astype(jnp.float32), axis=1).astype(jnp.int32)
    return (flat_ids * capacity + rank_in).reshape(route_ids.shape)


def head_split(matrix):
    return matrix.reshape(matrix.shape[0], -1, HEAD_DIM)


def attention_scores(queries, key_rows, score_bias, allowed):
    raw_scores = jnp.einsum(
        "qhd,khd->hqk",
        head_split(queries),
        head_split(key_rows),
        preferred_element_type=jnp.float32,
    )
    return jnp.where(allowed[None], raw_scores * HEAD_DIM ** (-0.5) + score_bias, -jnp.inf)


def to_experts(sent_rows, experts, capacity):
    row_width = sent_rows.shape[-1]
    repeated = jnp.broadcast_to(
        sent_rows.reshape(experts, 1, capacity, row_width), (experts, 4, capacity, row_width)
    )
    arrived = lax.all_to_all(
        repeated.reshape(experts * 4, capacity, row_width),
        "dp",
        split_axis=0,
        concat_axis=0,
        tiled=True,
    )
    gathered = arrived.reshape(-1, row_width)
    return gathered


def from_experts(part_rows, experts, capacity):
    row_width = part_rows.shape[-1]
    sources = part_rows.shape[0] // capacity
    returned_rows = lax.all_to_all(
        part_rows.reshape(sources, capacity, row_width),
        "dp",
        split_axis=0,
        concat_axis=0,
        tiled=True,
    )
    summed_rows = jnp.sum(
        returned_rows.reshape(experts, 4, capacity, row_width).astype(jnp.float32), axis=1
    ).reshape(experts * capacity, row_width)
    return summed_rows


def slot_rows(expert_rows, slot_index):
    selected = jnp.take(expert_rows, slot_index, axis=0)
    return selected


def on_device(
    tokens,
    seq_ids,
    routes,
    gain_attn,
    w_query,
    w_key,
    w_value,
    w_attn_out,
    rel_bias,
    gain_ffn,
    w_router,
    expert_in,
    expert_out,
    cotangent,
):
    tok_rows = tokens.shape[0]
    experts = w_router.shape[1]
    bucket_count = rel_bias.shape[1]
    capacity = 4 * ((5 * TOP * tok_rows + 16 * experts - 1) // (16 * experts))
    inputs_wide = tokens.astype(jnp.float32)
    normed_one, inv_one = rms_forward(inputs_wide, gain_attn)
    normed_one = normed_one.astype(jnp.bfloat16)
    queries = jnp.dot(normed_one, w_query, preferred_element_type=jnp.float32).astype(jnp.bfloat16)
    key_rows = jnp.dot(normed_one, w_key, preferred_element_type=jnp.float32).astype(jnp.bfloat16)
    value_rows = jnp.dot(normed_one, w_value, preferred_element_type=jnp.float32).astype(
        jnp.bfloat16
    )
    positions = jnp.arange(tok_rows)
    allowed = (seq_ids[:, None] == seq_ids[None, :]) & (positions[:, None] >= positions[None, :])
    bucket_hot = (
        jnp.asarray(bucket_matrix(tok_rows, bucket_count, REACH))[None]
        == jnp.arange(bucket_count, dtype=jnp.int32)[:, None, None]
    ).astype(jnp.float32)
    score_bias = jnp.einsum("hb,bij->hij", rel_bias, bucket_hot, precision=lax.Precision.HIGHEST)
    scores = attention_scores(queries, key_rows, score_bias, allowed)
    row_max = jnp.max(scores, axis=-1, keepdims=True)
    log_total = row_max + jnp.log(jnp.sum(jnp.exp(scores - row_max), axis=-1, keepdims=True))
    weights = jnp.exp(scores - log_total).astype(jnp.bfloat16)
    mixed_heads = (
        jnp.einsum(
            "hqk,khd->qhd", weights, head_split(value_rows), preferred_element_type=jnp.float32
        )
        .astype(jnp.bfloat16)
        .reshape(tok_rows, -1)
    )
    attended = lax.psum(
        jnp.dot(mixed_heads, w_attn_out, preferred_element_type=jnp.float32), "tensor"
    )
    residual_one = inputs_wide + attended
    normed_two, inv_two = rms_forward(residual_one, gain_ffn)
    normed_two = normed_two.astype(jnp.bfloat16)
    logits = jnp.dot(normed_two, w_router, preferred_element_type=jnp.float32)
    router_max = jnp.max(logits, axis=-1, keepdims=True)
    router_exp = jnp.exp(logits - router_max)
    router_probs = router_exp / jnp.sum(router_exp, axis=-1, keepdims=True)
    route_hot = (routes[:, :, None] == jnp.arange(experts, dtype=jnp.int32)[None, None, :]).astype(
        jnp.float32
    )
    gate_probs = jnp.sum(router_probs[:, None, :] * route_hot, axis=-1)
    slot_index = slot_of(routes, experts, capacity)
    pick_table = (
        slot_index[:, :, None] == jnp.arange(experts * capacity, dtype=jnp.int32)[None, None, :]
    ).astype(jnp.bfloat16)
    dispatched = jnp.einsum(
        "tks,td->sd", pick_table, normed_two, preferred_element_type=jnp.float32
    ).astype(jnp.bfloat16)
    received = to_experts(dispatched, experts, capacity)
    weight_in = expert_in[0]
    weight_out = expert_out[0]
    pre_act = jnp.dot(received, weight_in, preferred_element_type=jnp.float32)
    activated, gelu_back = jax.vjp(gelu_tanh, pre_act)
    activated = activated.astype(jnp.bfloat16)
    expert_part = jnp.dot(activated, weight_out, preferred_element_type=jnp.float32).astype(
        jnp.bfloat16
    )
    expert_rows = from_experts(expert_part, experts, capacity)
    chosen = slot_rows(expert_rows, slot_index)
    grad_wide = cotangent.astype(jnp.float32)
    mixture, grad_gate = lax.psum(
        (
            jnp.sum(gate_probs[:, :, None] * chosen, axis=1),
            jnp.sum(grad_wide[:, None, :] * chosen, axis=-1),
        ),
        "tensor",
    )
    output = (residual_one + mixture).astype(jnp.bfloat16)
    routed_grad = (gate_probs[:, :, None] * grad_wide[:, None, :]).astype(jnp.bfloat16)
    returned = jnp.einsum(
        "tks,tkd->sd", pick_table, routed_grad, preferred_element_type=jnp.float32
    ).astype(jnp.bfloat16)
    grad_rows = to_experts(returned, experts, capacity)
    grad_act = jnp.dot(grad_rows, weight_out.T, preferred_element_type=jnp.float32)
    grad_pre = gelu_back(grad_act)[0].astype(jnp.bfloat16)
    grad_weight_out = jnp.dot(activated.T, grad_rows, preferred_element_type=jnp.float32)
    grad_weight_in = jnp.dot(received.T, grad_pre, preferred_element_type=jnp.float32)
    back_part = jnp.dot(grad_pre, weight_in.T, preferred_element_type=jnp.float32).astype(
        jnp.bfloat16
    )
    back_rows = from_experts(back_part, experts, capacity)
    back_tokens = lax.psum(jnp.sum(slot_rows(back_rows, slot_index), axis=1), "tensor")
    grad_probs = jnp.sum(grad_gate[:, :, None] * route_hot, axis=1)
    grad_logits = (
        router_probs * (grad_probs - jnp.sum(router_probs * grad_probs, axis=-1, keepdims=True))
    ).astype(jnp.bfloat16)
    grad_router = jnp.dot(normed_two.T, grad_logits, preferred_element_type=jnp.float32)
    grad_normed_two = back_tokens + jnp.dot(
        grad_logits, w_router.T, preferred_element_type=jnp.float32
    )
    grad_res_norm, grad_gain_ffn = rms_backward(grad_normed_two, residual_one, inv_two, gain_ffn)
    grad_residual = grad_wide + grad_res_norm
    grad_attended = grad_residual.astype(jnp.bfloat16)
    grad_attn_out = jnp.dot(mixed_heads.T, grad_attended, preferred_element_type=jnp.float32)
    grad_mixed = jnp.dot(grad_attended, w_attn_out.T, preferred_element_type=jnp.float32).astype(
        jnp.bfloat16
    )
    scores_again = attention_scores(queries, key_rows, score_bias, allowed)
    probs_wide = jnp.exp(scores_again - log_total)
    grad_heads = head_split(grad_mixed)
    grad_values = (
        jnp.einsum(
            "hqk,qhd->khd",
            probs_wide.astype(jnp.bfloat16),
            grad_heads,
            preferred_element_type=jnp.float32,
        )
        .astype(jnp.bfloat16)
        .reshape(tok_rows, -1)
    )
    grad_probs_attn = jnp.einsum(
        "qhd,khd->hqk", grad_heads, head_split(value_rows), preferred_element_type=jnp.float32
    )
    delta_rows = jnp.sum(
        grad_heads.astype(jnp.float32) * head_split(mixed_heads).astype(jnp.float32), axis=-1
    ).T[:, :, None]
    grad_scores = probs_wide * (grad_probs_attn - delta_rows)
    grad_bias = jnp.einsum("hij,bij->hb", grad_scores, bucket_hot, precision=lax.Precision.HIGHEST)
    scores_half = grad_scores.astype(jnp.bfloat16)
    score_scale = HEAD_DIM ** (-0.5)
    grad_queries = (
        (
            jnp.einsum(
                "hqk,khd->qhd",
                scores_half,
                head_split(key_rows),
                preferred_element_type=jnp.float32,
            )
            * score_scale
        )
        .astype(jnp.bfloat16)
        .reshape(tok_rows, -1)
    )
    grad_keys = (
        (
            jnp.einsum(
                "hqk,qhd->khd", scores_half, head_split(queries), preferred_element_type=jnp.float32
            )
            * score_scale
        )
        .astype(jnp.bfloat16)
        .reshape(tok_rows, -1)
    )
    grad_query = jnp.dot(normed_one.T, grad_queries, preferred_element_type=jnp.float32)
    grad_key = jnp.dot(normed_one.T, grad_keys, preferred_element_type=jnp.float32)
    grad_value = jnp.dot(normed_one.T, grad_values, preferred_element_type=jnp.float32)
    grad_normed_part = jnp.dot(grad_queries, w_query.T, preferred_element_type=jnp.float32)
    grad_normed_part = grad_normed_part + jnp.dot(
        grad_keys, w_key.T, preferred_element_type=jnp.float32
    )
    grad_normed_part = grad_normed_part + jnp.dot(
        grad_values, w_value.T, preferred_element_type=jnp.float32
    )
    grad_normed_one = lax.psum(grad_normed_part.astype(jnp.bfloat16), "tensor").astype(jnp.float32)
    grad_in_norm, grad_gain_attn = rms_backward(grad_normed_one, inputs_wide, inv_one, gain_attn)
    grad_tokens = grad_residual + grad_in_norm
    summed = lax.psum(
        (
            grad_gain_attn,
            grad_query,
            grad_key,
            grad_value,
            grad_attn_out,
            grad_bias,
            grad_gain_ffn,
            grad_router,
        ),
        "dp",
    )
    return (
        output,
        grad_tokens,
        summed[0],
        summed[1],
        summed[2],
        summed[3],
        summed[4],
        summed[5],
        summed[6],
        summed[7],
        grad_weight_in[None],
        grad_weight_out[None],
    )


def solution(mesh):
    in_specs = (
        P("dp", None),
        P("dp"),
        P("dp", None),
        P(),
        P(None, "tensor"),
        P(None, "tensor"),
        P(None, "tensor"),
        P("tensor", None),
        P("tensor", None),
        P(),
        P(),
        P("dp", None, "tensor"),
        P("dp", "tensor", None),
        P("dp", None),
    )
    out_specs = (
        P("dp", None),
        P("dp", None),
        P(),
        P(None, "tensor"),
        P(None, "tensor"),
        P(None, "tensor"),
        P("tensor", None),
        P("tensor", None),
        P(),
        P(),
        P("dp", None, "tensor"),
        P("dp", "tensor", None),
    )
    return jax.shard_map(
        on_device, mesh=mesh, in_specs=in_specs, out_specs=out_specs, check_vma=False
    )
```

profile of v0, /device:TPU:0, one launch (start us, length us, event | category | flops | bytes accessed | tf_op | source)
XLA Modules:
  0.0 504.1 jit_solution(16210575287183119069)
XLA Ops:
  9.8 1.5 convolution_convert_fusion.5
  11.5 1.5 convolution_convert_fusion.4
  17.7 20.6 %all-reduce.8.cloned.1.call-done = f32[128,768]{1,0:T(8,128)} async-done(((f32[128,768]{1,0:T(8,128)}), f32[128,768]{1,0:T(8,128)}) %all-reduce.8.cloned.1.call-update) | async-done | bytes 393232 | tf_op jit(solution)/shard_map/psum | solution.py:154
  41.7 7.0 %all-to-all-start = ((bf16[16,80,768]{2,1,0:T(8,128)(2,1)}), bf16[16,80,768]{2,1,0:T(8,128)(2,1)}, u32[]{:S(2)}, u32[]{:S(2)}) async-start(bf16[16,80,768]{2,1,0:T(8,128)(2,1)} %bitcast.8), calls=%async_computation | async-start | bytes 3932160 | tf_op jit(solution)/shard_map/all_to_all | solution.py:76
  49.4 40.4 %all-to-all-done = bf16[16,80,768]{2,1,0:T(8,128)(2,1)} async-done(((bf16[16,80,768]{2,1,0:T(8,128)(2,1)}), bf16[16,80,768]{2,1,0:T(8,128)(2,1)}, u32[]{:S(2)}, u32[]{:S(2)}) %all-to-all-start) | async-done | bytes 1966112 | tf_op jit(solution)/shard_map/all_to_all | solution.py:76
  91.3 9.9 %all-to-all-start.2 = ((bf16[16,80,768]{2,1,0:T(8,128)(2,1)}), bf16[16,80,768]{2,1,0:T(8,128)(2,1)}, u32[]{:S(2)}, u32[]{:S(2)}) async-start(bf16[16,80,768]{2,1,0:T(8,128)(2,1)} %bitcast.17), calls=%async_computation.2 | async-start | bytes 3932160 | tf_op jit(solution)/shard_map/all_to_all | solution.py:76
  101.2 2.7 fusion.26
  105.2 2.9 convolution_convert_fusion.1
  108.1 33.6 %all-to-all-done.2 = bf16[16,80,768]{2,1,0:T(8,128)(2,1)} async-done(((bf16[16,80,768]{2,1,0:T(8,128)(2,1)}), bf16[16,80,768]{2,1,0:T(8,128)(2,1)}, u32[]{:S(2)}, u32[]{:S(2)}) %all-to-all-start.2) | async-done | bytes 1966112 | tf_op jit(solution)/shard_map/all_to_all | solution.py:76
  141.7 9.2 %all-to-all-start.1 = ((bf16[16,80,768]{2,1,0:T(8,128)(2,1)}), bf16[16,80,768]{2,1,0:T(8,128)(2,1)}, u32[]{:S(2)}, u32[]{:S(2)}) async-start(bf16[16,80,768]{2,1,0:T(8,128)(2,1)} %bitcast.105), calls=%async_computation.1 | async-start | bytes 3932160 | tf_op jit(solution)/shard_map/all_to_all | solution.py:90
  150.9 4.3 fusion.8
  156.2 2.5 convolution_convert_fusion
  158.6 32.7 %all-to-all-done.1 = bf16[16,80,768]{2,1,0:T(8,128)(2,1)} async-done(((bf16[16,80,768]{2,1,0:T(8,128)(2,1)}), bf16[16,80,768]{2,1,0:T(8,128)(2,1)}, u32[]{:S(2)}, u32[]{:S(2)}) %all-to-all-start.1) | async-done | bytes 1966112 | tf_op jit(solution)/shard_map/all_to_all | solution.py:90
  191.3 8.9 %all-to-all-start.3 = ((bf16[16,80,768]{2,1,0:T(8,128)(2,1)}), bf16[16,80,768]{2,1,0:T(8,128)(2,1)}, u32[]{:S(2)}, u32[]{:S(2)}) async-start(bf16[16,80,768]{2,1,0:T(8,128)(2,1)} %bitcast.104), calls=%async_computation.3 | async-start | bytes 3932160 | tf_op jit(solution)/shard_map/all_to_all | solution.py:90
  201.4 1.9 convert_reduce_fusion.1
  203.4 2.0 gather_fusion
  205.3 1.6 reshape.242
  207.9 32.5 %all-to-all-done.3 = bf16[16,80,768]{2,1,0:T(8,128)(2,1)} async-done(((bf16[16,80,768]{2,1,0:T(8,128)(2,1)}), bf16[16,80,768]{2,1,0:T(8,128)(2,1)}, u32[]{:S(2)}, u32[]{:S(2)}) %all-to-all-start.3) | async-done | bytes 1966112 | tf_op jit(solution)/shard_map/all_to_all | solution.py:90
  240.5 1.9 convert_reduce_fusion
  244.1 2.6 select_reduce_fusion
  246.8 2.6 psum.94
  249.4 20.1 %all-reduce.14.cloned.1.call-done = (f32[128,768]{1,0:T(8,128)}, f32[128,768]{1,0:T(8,128)}) async-done(((f32[128,768]{1,0:T(8,128)}, f32[128,768]{1,0:T(8,128)}), (f32[128,768]{1,0:T(8,128)}, f32[128,768]{1,0:T(8,128)})) %all-reduce.14.cloned.1.call-update) | async-done | bytes 786448 | tf_op jit(solution)/shard_map/psum | solution.py:187
  269.6 2.0 multiply_reduce_fusion.2
  271.6 1.7 subtract_add_fusion
  283.6 1.5 fusion.60
  286.2 3.9 convolution_bitcast_fusion.1
  290.2 3.7 convolution_bitcast_fusion
  295.4 7.5 %all-reduce.10.cloned.1.call-done = bf16[128,768]{1,0:T(8,128)(2,1)} async-done(((bf16[128,768]{1,0:T(8,128)(2,1)}), bf16[128,768]{1,0:T(8,128)(2,1)}) %all-reduce.10.cloned.1.call-update) | async-done | bytes 196624 | tf_op jit(solution)/shard_map/psum | solution.py:280
  304.0 79.7 %all-reduce = (f32[768]{0:T(1024)}, f32[6,32]{1,0:T(8,128)}, f32[768]{0:T(1024)}, f32[768,4]{0,1:T(4,128)}) all-reduce(f32[768]{0:T(1024)S(1)} %get-tuple-element.17, f32[6,32]{1,0:T(8,128)S(1)} %fusion.16, f32[768]{0:T(1024)S(1)} %copy-done.32, f32[768,4]{0,1:T(4,128)S(1)} %fusion.69), channel_id=1, replica_groups=mesh['dp'=16,'tensor'=2] {'dp'}, use_global_device_ids=true, to_apply=%region_25.27 | all-reduce | flops 4800 | bytes 38400 | tf_op jit(solution)/shard_map/psum | solution.py:283
  383.7 1.8 fusion.30
  385.6 106.5 %all-reduce.12.cloned.1.call-done = (f32[768,384]{1,0:T(8,128)}, f32[768,384]{1,0:T(8,128)}, f32[768,384]{1,0:T(8,128)}, f32[384,768]{1,0:T(8,128)}) async-done(((f32[768,384]{1,0:T(8,128)}, f32[768,384]{1,0:T(8,128)}, f32[768,384]{1,0:T(8,128)}, f32[384,768]{1,0:T(8,128)}), (f32[768,384]{1,0:T(8,128)}, f32[768,384]{1,0:T(8,128)}, f32[768,384]{1,0:T(8,128)}, ...) | async-done | bytes 4718608 | tf_op jit(solution)/shard_map/psum | solution.py:283
  492.0 2.5 copy.136
  (176 shorter events, 35.8 us)
Async XLA Ops:
  7.2 98.0 %copy-start = (bf16[1,384,768]{2,1,0:T(8,128)(2,1)S(1)}, bf16[1,384,768]{2,1,0:T(8,128)(2,1)}, u32[]{:S(2)}) copy-start(bf16[1,384,768]{2,1,0:T(8,128)(2,1)} %param.29) | copy-start | bytes 1769476
  7.2 6.5 %copy-start.19 = (s32[128,128]{1,0:T(8,128)S(1)}, s32[128,128]{1,0:T(8,128)}, u32[]{:S(2)}) copy-start(s32[128,128]{1,0:T(8,128)} %constant.43.clone) | copy-start | bytes 196612
  7.2 5.9 %copy-start.1 = (bf16[128,768]{1,0:T(8,128)(2,1)S(1)}, bf16[128,768]{1,0:T(8,128)(2,1)}, u32[]{:S(2)}) copy-start(bf16[128,768]{1,0:T(8,128)(2,1)} %param.17) | copy-start | bytes 589828
  7.2 5.9 %copy-start.18 = (f32[768]{0:T(1024)S(1)}, f32[768]{0:T(1024)}, u32[]{:S(2)}) copy-start(f32[768]{0:T(1024)} %param.20) | copy-start | bytes 9220
  7.2 5.9 %copy-start.2 = (bf16[768,384]{1,0:T(8,128)(2,1)S(1)}, bf16[768,384]{1,0:T(8,128)(2,1)}, u32[]{:S(2)}) copy-start(bf16[768,384]{1,0:T(8,128)(2,1)} %param.23) | copy-start | bytes 1769476
  7.2 6.4 %copy-start.42 = (f32[6,32]{1,0:T(8,128)S(1)}, f32[6,32]{1,0:T(8,128)}, u32[]{:S(2)}) copy-start(f32[6,32]{1,0:T(8,128)} %param.25) | copy-start | bytes 2308
  7.3 31.0 %all-reduce.8.cloned.1.call-start = ((), (), s32[]{:S(2)}) async-start(), calls=%async_computation.4 | async-start | bytes 786432 | tf_op jit(solution)/shard_map/psum | solution.py:154
  14.9 25.0 %copy-start.21 = (f32[768]{0:T(1024)S(1)}, f32[768]{0:T(1024)}, u32[]{:S(2)}) copy-start(f32[768]{0:T(1024)} %param.26) | copy-start | bytes 9220
  41.7 7.0 %copy-start.16 = (bf16[128,768]{1,0:T(8,128)(2,1)S(1)}, bf16[128,768]{1,0:T(8,128)(2,1)}, u32[]{:S(2)}) copy-start(bf16[128,768]{1,0:T(8,128)(2,1)} %param.30) | copy-start | bytes 589828
  41.7 7.0 %copy-start.27 = (bf16[768,4]{0,1:T(4,128)(2,1)S(1)}, bf16[768,4]{0,1:T(4,128)(2,1)}, u32[]{:S(2)}) copy-start(bf16[768,4]{0,1:T(4,128)(2,1)} %param.27) | copy-start | bytes 18436
  41.7 48.1 %all-to-all-start = ((bf16[16,80,768]{2,1,0:T(8,128)(2,1)}), bf16[16,80,768]{2,1,0:T(8,128)(2,1)}, u32[]{:S(2)}, u32[]{:S(2)}) async-start(bf16[16,80,768]{2,1,0:T(8,128)(2,1)} %bitcast.8), calls=%async_computation | async-start | bytes 3932160 | tf_op jit(solution)/shard_map/all_to_all | solution.py:76
  48.9 42.4 %copy-start.29 = (f32[128]{0:T(128)}, f32[128]{0:T(128)S(1)}, u32[]{:S(2)}) copy-start(f32[128]{0:T(128)S(1)} %get-tuple-element.41) | copy-start | bytes 1540
  49.0 42.3 %copy-start.35 = (f32[128]{0:T(128)}, f32[128]{0:T(128)S(1)}, u32[]{:S(2)}) copy-start(f32[128]{0:T(128)S(1)} %fusion.55) | copy-start | bytes 1540
  91.2 9.9 %copy-start.46 = (bf16[1,768,384]{2,1,0:T(8,128)(2,1)S(1)}, bf16[1,768,384]{2,1,0:T(8,128)(2,1)}, u32[]{:S(2)}) copy-start(bf16[1,768,384]{2,1,0:T(8,128)(2,1)} %param.28) | copy-start | bytes 1769476
  91.3 50.4 %all-to-all-start.2 = ((bf16[16,80,768]{2,1,0:T(8,128)(2,1)}), bf16[16,80,768]{2,1,0:T(8,128)(2,1)}, u32[]{:S(2)}, u32[]{:S(2)}) async-start(bf16[16,80,768]{2,1,0:T(8,128)(2,1)} %bitcast.17), calls=%async_computation.2 | async-start | bytes 3932160 | tf_op jit(solution)/shard_map/all_to_all | solution.py:76
  141.7 49.6 %all-to-all-start.1 = ((bf16[16,80,768]{2,1,0:T(8,128)(2,1)}), bf16[16,80,768]{2,1,0:T(8,128)(2,1)}, u32[]{:S(2)}, u32[]{:S(2)}) async-start(bf16[16,80,768]{2,1,0:T(8,128)(2,1)} %bitcast.105), calls=%async_computation.1 | async-start | bytes 3932160 | tf_op jit(solution)/shard_map/all_to_all | solution.py:90
  191.3 49.1 %all-to-all-start.3 = ((bf16[16,80,768]{2,1,0:T(8,128)(2,1)}), bf16[16,80,768]{2,1,0:T(8,128)(2,1)}, u32[]{:S(2)}, u32[]{:S(2)}) async-start(bf16[16,80,768]{2,1,0:T(8,128)(2,1)} %bitcast.104), calls=%async_computation.3 | async-start | bytes 3932160 | tf_op jit(solution)/shard_map/all_to_all | solution.py:90
  200.2 69.3 %all-reduce.14.cloned.1.call-start = ((), (), s32[]{:S(2)}) async-start(), calls=%async_computation.7 | async-start | bytes 1572864 | tf_op jit(solution)/shard_map/psum | solution.py:187
  244.0 5.4 %copy-start.30 = (f32[128]{0:T(128)S(1)}, f32[128]{0:T(128)}, u32[]{:S(2)}) copy-start(f32[128]{0:T(128)} %copy-done.29) | copy-start | bytes 1540
  244.0 5.4 %copy-start.36 = (f32[128]{0:T(128)S(1)}, f32[128]{0:T(128)}, u32[]{:S(2)}) copy-start(f32[128]{0:T(128)} %copy-done.35) | copy-start | bytes 1540
  244.0 25.5 %copy-start.22 = (f32[768]{0:T(1024)S(1)}, f32[768]{0:T(1024)}, u32[]{:S(2)}) copy-start(f32[768]{0:T(1024)} %param.26) | copy-start | bytes 9220
  244.0 25.5 %copy-start.28 = (bf16[768,4]{0,1:T(4,128)(2,1)S(1)}, bf16[768,4]{0,1:T(4,128)(2,1)}, u32[]{:S(2)}) copy-start(bf16[768,4]{0,1:T(4,128)(2,1)} %param.27) | copy-start | bytes 18436
  244.0 25.5 %copy-start.41 = (f32[128]{0:T(128)S(1)}, f32[128]{0:T(128)}, u32[]{:S(2)}) copy-start(f32[128]{0:T(128)} %copy-done.40) | copy-start | bytes 1540
  244.0 27.5 %copy-start.17 = (bf16[128,768]{1,0:T(8,128)(2,1)S(1)}, bf16[128,768]{1,0:T(8,128)(2,1)}, u32[]{:S(2)}) copy-start(bf16[128,768]{1,0:T(8,128)(2,1)} %param.30) | copy-start | bytes 589828
  244.1 27.5 %copy-start.45 = (f32[128]{0:T(128)S(1)}, f32[128]{0:T(128)}, u32[]{:S(2)}) copy-start(f32[128]{0:T(128)} %get-tuple-element.37) | copy-start | bytes 1540
  246.7 26.6 %copy-start.5 = (bf16[384,768]{1,0:T(8,128)(2,1)S(1)}, bf16[384,768]{1,0:T(8,128)(2,1)}, u32[]{:S(2)}) copy-start(bf16[384,768]{1,0:T(8,128)(2,1)} %param.24) | copy-start | bytes 1769476
  246.7 56.2 %all-reduce.10.cloned.1.call-start = ((), (), s32[]{:S(2)}) async-start(), calls=%async_computation.5 | async-start | bytes 393216 | tf_op jit(solution)/shard_map/psum | solution.py:280
  249.4 23.9 %copy-start.25 = (f32[128,4]{0,1:T(4,128)}, f32[128,4]{0,1:T(4,128)S(1)}, u32[]{:S(2)}) copy-start(f32[128,4]{0,1:T(4,128)S(1)} %select_reduce_fusion.1) | copy-start | bytes 6148
  249.4 23.9 %copy-start.38 = (f32[128]{0:T(128)}, f32[128]{0:T(128)S(1)}, u32[]{:S(2)}) copy-start(f32[128]{0:T(128)S(1)} %multiply_reduce_fusion.6) | copy-start | bytes 1540
  283.5 208.5 %all-reduce.12.cloned.1.call-start = ((), (), s32[]{:S(2)}) async-start(), calls=%async_computation.6 | async-start | bytes 9437184 | tf_op jit(solution)/shard_map/psum | solution.py:283
  293.9 10.1 %copy-start.32 = (f32[768]{0:T(1024)S(1)}, f32[768]{0:T(1024)}, u32[]{:S(2)}) copy-start(f32[768]{0:T(1024)} %get-tuple-element.15) | copy-start | bytes 9220
  293.9 89.8 %copy-start.44 = (f32[128]{0:T(128)S(1)}, f32[128]{0:T(128)}, u32[]{:S(2)}) copy-start(f32[128]{0:T(128)} %get-tuple-element.35) | copy-start | bytes 1540
  (27 other events, 81.9 us)
Sparse Core Ops, SparseCore 0:
  17.1 21.1 all-reduce.7
  246.8 22.6 all-reduce.13
  283.6 19.2 all-reduce.9
  309.4 182.6 all-reduce.11
where the time goes:
time: 505 us; the launch traced here: 504 us
  waiting for transfers between devices  294 us (58%)
  blocking collectives  82.3 us (16%)
  matrix products  41.1 us (8%)
  starting transfers between devices  35.3 us (7%)
  local copies, waits for them, and re-layouts  20.1 us (4%)
  other arithmetic  16.8 us (3%)
  between operations  14.6 us (3%)
    psum x1, waiting for transfers between devices, on_device(): lax.psum((grad_gain_attn, grad_query, grad_key, grad_value, grad_attn_out...  106 us
    psum x1, blocking collectives, on_device(): lax.psum((grad_gain_attn, grad_query, grad_key, grad_value, grad_attn_out...  79.7 us
    all_to_all x2, waiting for transfers between devices, to_experts(): lax.all_to_all(repeated.reshape(experts * 4, capacity, row_width), 'dp',...  74.1 us
    all_to_all x2, waiting for transfers between devices, from_experts(): lax.all_to_all(part_rows.reshape(sources, capacity, row_width), 'dp', spl...  65.2 us
    psum x1, waiting for transfers between devices, on_device(): lax.psum(jnp.dot(mixed_heads, w_attn_out, preferred_element_type=jnp.floa...  20.6 us
    psum x1, waiting for transfers between devices, on_device(): lax.psum((jnp.sum(gate_probs[:, :, None] * chosen, axis=1), jnp.sum(grad_...  20.1 us
    all_to_all x2, starting transfers between devices, from_experts(): lax.all_to_all(part_rows.reshape(sources, capacity, row_width), 'dp', spl...  18 us
    all_to_all x2, starting transfers between devices, to_experts(): lax.all_to_all(repeated.reshape(experts * 4, capacity, row_width), 'dp',...  16.9 us
  transfers between devices with their start and end apart: 8, of which 8 were waited for; matrix products, arithmetic and copies ran while one was open for 7% of the time, Pallas kernels for 0%

commit v1 on v0

--- a/solution.py
+++ b/solution.py
@@ -151,8 +151,11 @@
         .astype(jnp.bfloat16)
         .reshape(tok_rows, -1)
     )
-    attended = lax.psum(
-        jnp.dot(mixed_heads, w_attn_out, preferred_element_type=jnp.float32), "tensor"
+    attended = jnp.sum(
+        lax.all_gather(
+            jnp.dot(mixed_heads, w_attn_out, preferred_element_type=jnp.float32), "tensor"
+        ),
+        axis=0,
     )
     residual_one = inputs_wide + attended
     normed_two, inv_two = rms_forward(residual_one, gain_ffn)

time: 505 us -> 488 us (0.966)
  waiting for transfers between devices: 294 us -> 275 us
    psum x1 -> x0, waiting for transfers between devices: 20.6 us -> none  [on_device(): lax.psum(jnp.dot(mixed_heads, w_attn_out, preferred_element_type=jnp.floa...]
  transfers between devices with their start and end apart: 8 -> 7, of which waited for: 8 -> 7; matrix products, arithmetic and copies ran while one was open for 7% -> 7% of each run, Pallas kernels for 0% -> 0%
where the time goes in v1:
time: 488 us
  waiting for transfers between devices  275 us (56%)
  blocking collectives  84.6 us (17%)
  matrix products  40.4 us (8%)
  starting transfers between devices  36.4 us (7%)
  local copies, waits for them, and re-layouts  20.5 us (4%)
  other arithmetic  16.5 us (3%)
  between operations  14.5 us (3%)
    psum x1, waiting for transfers between devices, on_device(): lax.psum((grad_gain_attn, grad_query, grad_key, grad_value, grad_attn_out...  108 us
    psum x1, blocking collectives, on_device(): lax.psum((grad_gain_attn, grad_query, grad_key, grad_value, grad_attn_out...  79.6 us
    all_to_all x2, waiting for transfers between devices, to_experts(): lax.all_to_all(repeated.reshape(experts * 4, capacity, row_width), 'dp',...  74 us
    all_to_all x2, waiting for transfers between devices, from_experts(): lax.all_to_all(part_rows.reshape(sources, capacity, row_width), 'dp', spl...  65.2 us
    psum x1, waiting for transfers between devices, on_device(): lax.psum((jnp.sum(gate_probs[:, :, None] * chosen, axis=1), jnp.sum(grad_...  20.1 us
    all_to_all x2, starting transfers between devices, to_experts(): lax.all_to_all(repeated.reshape(experts * 4, capacity, row_width), 'dp',...  18.1 us
    all_to_all x2, starting transfers between devices, from_experts(): lax.all_to_all(part_rows.reshape(sources, capacity, row_width), 'dp', spl...  18 us
    unnamed x107, local copies, waits for them, and re-layouts  10.3 us
  transfers between devices with their start and end apart: 7, of which 7 were waited for; matrix products, arithmetic and copies ran while one was open for 7% of the time, Pallas kernels for 0%

profile of v1, /device:TPU:0, one launch (start us, length us, event | category | flops | bytes accessed | tf_op | source)
XLA Modules:
  0.0 487.5 jit_solution(14146158456611691396)
XLA Ops:
  11.9 1.5 convolution_convert_fusion.5
  13.5 1.5 convolution_convert_fusion.4
  17.9 2.4 all-gather
  22.8 8.4 %all-to-all-start = ((bf16[16,80,768]{2,1,0:T(8,128)(2,1)}), bf16[16,80,768]{2,1,0:T(8,128)(2,1)}, u32[]{:S(2)}, u32[]{:S(2)}) async-start(bf16[16,80,768]{2,1,0:T(8,128)(2,1)} %bitcast.9), calls=%async_computation | async-start | bytes 3932160 | tf_op jit(solution)/shard_map/all_to_all | solution.py:76
  32.0 40.5 %all-to-all-done = bf16[16,80,768]{2,1,0:T(8,128)(2,1)} async-done(((bf16[16,80,768]{2,1,0:T(8,128)(2,1)}), bf16[16,80,768]{2,1,0:T(8,128)(2,1)}, u32[]{:S(2)}, u32[]{:S(2)}) %all-to-all-start) | async-done | bytes 1966112 | tf_op jit(solution)/shard_map/all_to_all | solution.py:76
  73.9 9.6 %all-to-all-start.2 = ((bf16[16,80,768]{2,1,0:T(8,128)(2,1)}), bf16[16,80,768]{2,1,0:T(8,128)(2,1)}, u32[]{:S(2)}, u32[]{:S(2)}) async-start(bf16[16,80,768]{2,1,0:T(8,128)(2,1)} %bitcast.18), calls=%async_computation.2 | async-start | bytes 3932160 | tf_op jit(solution)/shard_map/all_to_all | solution.py:76
  83.5 2.7 fusion.26
  87.6 2.9 convolution_convert_fusion.1
  90.4 33.5 %all-to-all-done.2 = bf16[16,80,768]{2,1,0:T(8,128)(2,1)} async-done(((bf16[16,80,768]{2,1,0:T(8,128)(2,1)}), bf16[16,80,768]{2,1,0:T(8,128)(2,1)}, u32[]{:S(2)}, u32[]{:S(2)}) %all-to-all-start.2) | async-done | bytes 1966112 | tf_op jit(solution)/shard_map/all_to_all | solution.py:76
  124.0 9.2 %all-to-all-start.1 = ((bf16[16,80,768]{2,1,0:T(8,128)(2,1)}), bf16[16,80,768]{2,1,0:T(8,128)(2,1)}, u32[]{:S(2)}, u32[]{:S(2)}) async-start(bf16[16,80,768]{2,1,0:T(8,128)(2,1)} %bitcast.107), calls=%async_computation.1 | async-start | bytes 3932160 | tf_op jit(solution)/shard_map/all_to_all | solution.py:90
  133.1 4.3 fusion.8
  138.4 2.5 convolution_convert_fusion
  140.9 32.7 %all-to-all-done.1 = bf16[16,80,768]{2,1,0:T(8,128)(2,1)} async-done(((bf16[16,80,768]{2,1,0:T(8,128)(2,1)}), bf16[16,80,768]{2,1,0:T(8,128)(2,1)}, u32[]{:S(2)}, u32[]{:S(2)}) %all-to-all-start.1) | async-done | bytes 1966112 | tf_op jit(solution)/shard_map/all_to_all | solution.py:90
  173.6 8.9 %all-to-all-start.3 = ((bf16[16,80,768]{2,1,0:T(8,128)(2,1)}), bf16[16,80,768]{2,1,0:T(8,128)(2,1)}, u32[]{:S(2)}, u32[]{:S(2)}) async-start(bf16[16,80,768]{2,1,0:T(8,128)(2,1)} %bitcast.106), calls=%async_computation.3 | async-start | bytes 3932160 | tf_op jit(solution)/shard_map/all_to_all | solution.py:90
  183.7 1.9 convert_reduce_fusion.1
  185.6 2.0 gather_fusion
  187.6 1.6 reshape.243
  190.2 32.5 %all-to-all-done.3 = bf16[16,80,768]{2,1,0:T(8,128)(2,1)} async-done(((bf16[16,80,768]{2,1,0:T(8,128)(2,1)}), bf16[16,80,768]{2,1,0:T(8,128)(2,1)}, u32[]{:S(2)}, u32[]{:S(2)}) %all-to-all-start.3) | async-done | bytes 1966112 | tf_op jit(solution)/shard_map/all_to_all | solution.py:90
  222.7 1.9 convert_reduce_fusion
  226.3 2.6 select_reduce_fusion
  229.0 2.6 psum.86
  231.7 20.1 %all-reduce.11.cloned.1.call-done = (f32[128,768]{1,0:T(8,128)}, f32[128,768]{1,0:T(8,128)}) async-done(((f32[128,768]{1,0:T(8,128)}, f32[128,768]{1,0:T(8,128)}), (f32[128,768]{1,0:T(8,128)}, f32[128,768]{1,0:T(8,128)})) %all-reduce.11.cloned.1.call-update) | async-done | bytes 786448 | tf_op jit(solution)/shard_map/psum | solution.py:190
  251.8 2.0 multiply_reduce_fusion.2
  253.8 1.7 subtract_add_fusion
  261.5 1.5 fusion.58
  268.5 3.9 convolution_bitcast_fusion.1
  272.4 3.7 convolution_bitcast_fusion
  277.6 7.5 %all-reduce.7.cloned.1.call-done = bf16[128,768]{1,0:T(8,128)(2,1)} async-done(((bf16[128,768]{1,0:T(8,128)(2,1)}), bf16[128,768]{1,0:T(8,128)(2,1)}) %all-reduce.7.cloned.1.call-update) | async-done | bytes 196624 | tf_op jit(solution)/shard_map/psum | solution.py:283
  286.3 79.6 %all-reduce = (f32[768]{0:T(1024)}, f32[6,32]{1,0:T(8,128)}, f32[768]{0:T(1024)}, f32[768,4]{0,1:T(4,128)}) all-reduce(f32[768]{0:T(1024)S(1)} %get-tuple-element.17, f32[6,32]{1,0:T(8,128)S(1)} %fusion.16, f32[768]{0:T(1024)S(1)} %copy-done.32, f32[768,4]{0,1:T(4,128)S(1)} %fusion.69), channel_id=1, replica_groups=mesh['dp'=16,'tensor'=2] {'dp'}, use_global_device_ids=true, to_apply=%region_25.27 | all-reduce | flops 4800 | bytes 38400 | tf_op jit(solution)/shard_map/psum | solution.py:286
  365.9 1.8 fusion.30
  367.7 107.7 %all-reduce.9.cloned.1.call-done = (f32[768,384]{1,0:T(8,128)}, f32[768,384]{1,0:T(8,128)}, f32[768,384]{1,0:T(8,128)}, f32[384,768]{1,0:T(8,128)}) async-done(((f32[768,384]{1,0:T(8,128)}, f32[768,384]{1,0:T(8,128)}, f32[768,384]{1,0:T(8,128)}, f32[384,768]{1,0:T(8,128)}), (f32[768,384]{1,0:T(8,128)}, f32[768,384]{1,0:T(8,128)}, f32[768,384]{1,0:T(8,128)}, ...) | async-done | bytes 4718608 | tf_op jit(solution)/shard_map/psum | solution.py:286
  475.4 2.5 copy.135
  (175 shorter events, 35.1 us)
Async XLA Ops:
  7.2 80.4 %copy-start = (bf16[1,384,768]{2,1,0:T(8,128)(2,1)S(1)}, bf16[1,384,768]{2,1,0:T(8,128)(2,1)}, u32[]{:S(2)}) copy-start(bf16[1,384,768]{2,1,0:T(8,128)(2,1)} %param.29) | copy-start | bytes 1769476
  7.2 8.5 %copy-start.19 = (s32[128,128]{1,0:T(8,128)S(1)}, s32[128,128]{1,0:T(8,128)}, u32[]{:S(2)}) copy-start(s32[128,128]{1,0:T(8,128)} %constant.43.clone) | copy-start | bytes 196612
  7.2 8.0 %copy-start.1 = (bf16[128,768]{1,0:T(8,128)(2,1)S(1)}, bf16[128,768]{1,0:T(8,128)(2,1)}, u32[]{:S(2)}) copy-start(bf16[128,768]{1,0:T(8,128)(2,1)} %param.17) | copy-start | bytes 589828
  7.2 8.0 %copy-start.18 = (f32[768]{0:T(1024)S(1)}, f32[768]{0:T(1024)}, u32[]{:S(2)}) copy-start(f32[768]{0:T(1024)} %param.20) | copy-start | bytes 9220
  7.2 8.0 %copy-start.2 = (bf16[768,384]{1,0:T(8,128)(2,1)S(1)}, bf16[768,384]{1,0:T(8,128)(2,1)}, u32[]{:S(2)}) copy-start(bf16[768,384]{1,0:T(8,128)(2,1)} %param.23) | copy-start | bytes 1769476
  7.2 8.4 %copy-start.42 = (f32[6,32]{1,0:T(8,128)S(1)}, f32[6,32]{1,0:T(8,128)}, u32[]{:S(2)}) copy-start(f32[6,32]{1,0:T(8,128)} %param.25) | copy-start | bytes 2308
  8.9 7.5 %copy-start.23 = (f32[128]{0:T(128)}, f32[128]{0:T(128)S(1)}, u32[]{:S(2)}) copy-start(f32[128]{0:T(128)S(1)} %get-tuple-element.36) | copy-start | bytes 1540
  22.8 8.5 %copy-start.16 = (bf16[128,768]{1,0:T(8,128)(2,1)S(1)}, bf16[128,768]{1,0:T(8,128)(2,1)}, u32[]{:S(2)}) copy-start(bf16[128,768]{1,0:T(8,128)(2,1)} %param.30) | copy-start | bytes 589828
  22.8 8.5 %copy-start.27 = (bf16[768,4]{0,1:T(4,128)(2,1)S(1)}, bf16[768,4]{0,1:T(4,128)(2,1)}, u32[]{:S(2)}) copy-start(bf16[768,4]{0,1:T(4,128)(2,1)} %param.27) | copy-start | bytes 18436
  22.8 8.8 %copy-start.33 = (s32[128,2]{0,1:T(2,128)S(1)}, s32[128,2]{0,1:T(2,128)}, u32[]{:S(2)}) copy-start(s32[128,2]{0,1:T(2,128)} %param.19) | copy-start | bytes 3076
  22.8 49.6 %all-to-all-start = ((bf16[16,80,768]{2,1,0:T(8,128)(2,1)}), bf16[16,80,768]{2,1,0:T(8,128)(2,1)}, u32[]{:S(2)}, u32[]{:S(2)}) async-start(bf16[16,80,768]{2,1,0:T(8,128)(2,1)} %bitcast.9), calls=%async_computation | async-start | bytes 3932160 | tf_op jit(solution)/shard_map/all_to_all | solution.py:76
  31.5 42.4 %copy-start.29 = (f32[128]{0:T(128)}, f32[128]{0:T(128)S(1)}, u32[]{:S(2)}) copy-start(f32[128]{0:T(128)S(1)} %get-tuple-element.41) | copy-start | bytes 1540
  31.5 42.3 %copy-start.35 = (f32[128]{0:T(128)}, f32[128]{0:T(128)S(1)}, u32[]{:S(2)}) copy-start(f32[128]{0:T(128)S(1)} %fusion.55) | copy-start | bytes 1540
  73.9 9.7 %copy-start.46 = (bf16[1,768,384]{2,1,0:T(8,128)(2,1)S(1)}, bf16[1,768,384]{2,1,0:T(8,128)(2,1)}, u32[]{:S(2)}) copy-start(bf16[1,768,384]{2,1,0:T(8,128)(2,1)} %param.28) | copy-start | bytes 1769476
  73.9 50.1 %all-to-all-start.2 = ((bf16[16,80,768]{2,1,0:T(8,128)(2,1)}), bf16[16,80,768]{2,1,0:T(8,128)(2,1)}, u32[]{:S(2)}, u32[]{:S(2)}) async-start(bf16[16,80,768]{2,1,0:T(8,128)(2,1)} %bitcast.18), calls=%async_computation.2 | async-start | bytes 3932160 | tf_op jit(solution)/shard_map/all_to_all | solution.py:76
  124.0 49.6 %all-to-all-start.1 = ((bf16[16,80,768]{2,1,0:T(8,128)(2,1)}), bf16[16,80,768]{2,1,0:T(8,128)(2,1)}, u32[]{:S(2)}, u32[]{:S(2)}) async-start(bf16[16,80,768]{2,1,0:T(8,128)(2,1)} %bitcast.107), calls=%async_computation.1 | async-start | bytes 3932160 | tf_op jit(solution)/shard_map/all_to_all | solution.py:90
  173.6 49.1 %all-to-all-start.3 = ((bf16[16,80,768]{2,1,0:T(8,128)(2,1)}), bf16[16,80,768]{2,1,0:T(8,128)(2,1)}, u32[]{:S(2)}, u32[]{:S(2)}) async-start(bf16[16,80,768]{2,1,0:T(8,128)(2,1)} %bitcast.106), calls=%async_computation.3 | async-start | bytes 3932160 | tf_op jit(solution)/shard_map/all_to_all | solution.py:90
  182.5 69.3 %all-reduce.11.cloned.1.call-start = ((), (), s32[]{:S(2)}) async-start(), calls=%async_computation.6 | async-start | bytes 1572864 | tf_op jit(solution)/shard_map/psum | solution.py:190
  226.2 5.4 %copy-start.34 = (s32[128,2]{0,1:T(2,128)S(1)}, s32[128,2]{0,1:T(2,128)}, u32[]{:S(2)}) copy-start(s32[128,2]{0,1:T(2,128)} %param.19) | copy-start | bytes 3076
  226.2 5.4 %copy-start.30 = (f32[128]{0:T(128)S(1)}, f32[128]{0:T(128)}, u32[]{:S(2)}) copy-start(f32[128]{0:T(128)} %copy-done.29) | copy-start | bytes 1540
  226.3 25.5 %copy-start.22 = (f32[768]{0:T(1024)S(1)}, f32[768]{0:T(1024)}, u32[]{:S(2)}) copy-start(f32[768]{0:T(1024)} %param.26) | copy-start | bytes 9220
  226.3 25.5 %copy-start.28 = (bf16[768,4]{0,1:T(4,128)(2,1)S(1)}, bf16[768,4]{0,1:T(4,128)(2,1)}, u32[]{:S(2)}) copy-start(bf16[768,4]{0,1:T(4,128)(2,1)} %param.27) | copy-start | bytes 18436
  226.3 25.5 %copy-start.41 = (f32[128]{0:T(128)S(1)}, f32[128]{0:T(128)}, u32[]{:S(2)}) copy-start(f32[128]{0:T(128)} %copy-done.40) | copy-start | bytes 1540
  226.3 27.5 %copy-start.17 = (bf16[128,768]{1,0:T(8,128)(2,1)S(1)}, bf16[128,768]{1,0:T(8,128)(2,1)}, u32[]{:S(2)}) copy-start(bf16[128,768]{1,0:T(8,128)(2,1)} %param.30) | copy-start | bytes 589828
  226.3 27.5 %copy-start.45 = (f32[128]{0:T(128)S(1)}, f32[128]{0:T(128)}, u32[]{:S(2)}) copy-start(f32[128]{0:T(128)} %get-tuple-element.37) | copy-start | bytes 1540
  228.9 26.6 %copy-start.5 = (bf16[384,768]{1,0:T(8,128)(2,1)S(1)}, bf16[384,768]{1,0:T(8,128)(2,1)}, u32[]{:S(2)}) copy-start(bf16[384,768]{1,0:T(8,128)(2,1)} %param.24) | copy-start | bytes 1769476
  229.0 56.2 %all-reduce.7.cloned.1.call-start = ((), (), s32[]{:S(2)}) async-start(), calls=%async_computation.4 | async-start | bytes 393216 | tf_op jit(solution)/shard_map/psum | solution.py:283
  231.7 23.9 %copy-start.25 = (f32[128,4]{0,1:T(4,128)}, f32[128,4]{0,1:T(4,128)S(1)}, u32[]{:S(2)}) copy-start(f32[128,4]{0,1:T(4,128)S(1)} %select_reduce_fusion.1) | copy-start | bytes 6148
  231.7 23.9 %copy-start.38 = (f32[128]{0:T(128)}, f32[128]{0:T(128)S(1)}, u32[]{:S(2)}) copy-start(f32[128]{0:T(128)S(1)} %multiply_reduce_fusion.6) | copy-start | bytes 1540
  265.8 209.6 %all-reduce.9.cloned.1.call-start = ((), (), s32[]{:S(2)}) async-start(), calls=%async_computation.5 | async-start | bytes 9437184 | tf_op jit(solution)/shard_map/psum | solution.py:286
  276.1 10.1 %copy-start.32 = (f32[768]{0:T(1024)S(1)}, f32[768]{0:T(1024)}, u32[]{:S(2)}) copy-start(f32[768]{0:T(1024)} %get-tuple-element.15) | copy-start | bytes 9220
  276.2 89.7 %copy-start.44 = (f32[128]{0:T(128)S(1)}, f32[128]{0:T(128)}, u32[]{:S(2)}) copy-start(f32[128]{0:T(128)} %get-tuple-element.35) | copy-start | bytes 1540
  (26 other events, 77.2 us)
Sparse Core Ops, SparseCore 0:
  229.1 22.6 all-reduce.10
  265.9 19.2 all-reduce.6
  292.8 182.5 all-reduce.8
